TPU v7x, 512 devices: a whole 4x4x16 slice. The times are simulated.
512 devices in a mesh: snap: 16 (over y, x), plane: 32 (over z, core).
Axes of the slice: x: 4, y: 4, z: 16, core: 2. Of those that a mesh axis runs over, the one named last changes fastest.
Arguments:
- velocity: bfloat16 [16, 128, 3, 128, 128], P('snap', 'plane'), may hold values from -6 to 6
- plane_count: int32 [32], P('plane'), may hold values from 1 to 4, as said below
- inv_span: float32 [32, 4], P('plane'), may hold values from 0.5 to 4
- kernels: float32 [3, 2, 3, 3], replicated, may hold values from -2.4 to 2.4
- omega_block: int32 [32, 4], P('plane'), may hold values from 0 to 7
- omega_table: bfloat16 [8, 9, 32, 256], replicated, may hold values from -0.0625 to 0.0625
- omega_stream: bfloat16 [32, 256], replicated, may hold values from -6 to 6
- wall_shear: bfloat16 [16, 2, 128, 128], P('snap', None, 'plane'), may hold values from -6 to 6
Outputs:
- sketch: float32 [2, 32, 32, 256], P(None, 'plane', 'snap')
- gram: float32 [256, 256], replicated
Inputs may be any that keep to these rules, and one draw needn't show every extreme that they name: `plane_count`: every index of plane holds 1 or more live slots, slots 0 onwards; some index holds 4.
All inputs are finite; a program needn't handle non-finite values.
Results may differ from a plain program's by a relative error of at most 0.0043.
Values may be sent and summed in bfloat16 or wider, within the bound.
No kernel may reach another device: no remote copies, remote signals or barrier semaphores. Data moves between devices by JAX's collectives and lax.ppermute only.
A program may use at most 64 MiB of HBM per device.

v0:
```python
import jax
import jax.numpy as jnp
from jax import lax
from jax.sharding import PartitionSpec as P

X = 128
ZW = 128


def shifted(value, axis, steps):
    count = lax.axis_size(axis)
    leading, last = (max(0, -steps), min(count, count - steps))
    return lax.ppermute(value, axis, [(source, source + steps) for source in range(leading, last)])


def in_plane(centre, kernels):
    snaps, comps, zw, xw = centre.shape
    field = centre.astype(jnp.float32)
    padded = jnp.pad(field, ((0, 0), (0, 0), (1, 1), (1, 1)))
    first = jnp.zeros_like(field)
    second = jnp.zeros_like(field)
    for row_a in range(3):
        for col_b in range(3):
            window = padded[:, :, row_a : row_a + zw, col_b : col_b + xw]
            first = first + kernels[:, 0, row_a, col_b][None, :, None, None] * window
            second = second + kernels[:, 1, row_a, col_b][None, :, None, None] * window
    return (first, second)


def features(centre, below, above, span, kernels):
    snaps, comps, zw, xw = centre.shape
    first, second = in_plane(centre, kernels)
    normal = (above.astype(jnp.float32) - below.astype(jnp.float32)) * span
    grads = jnp.stack([first, second, normal], axis=2).reshape(snaps, 9, zw, xw)
    filtered = grads.reshape(snaps, 9, zw // 4, 4, xw // 4, 4).mean(axis=(3, 5))
    return filtered.astype(jnp.bfloat16)


def per_device(
    velocity, plane_count, inv_span, kernels, omega_block, omega_table, omega_stream, wall_shear
):
    slots = velocity.shape[1]
    live_count = plane_count[0]
    coef = jnp.zeros((velocity.shape[0], omega_stream.shape[1]), jnp.float32)
    last_live = lax.dynamic_index_in_dim(velocity, live_count - 1, 1, keepdims=False)
    from_below = shifted(last_live, "plane", 1)
    from_above = shifted(velocity[:, 0], "plane", -1)
    for slot in range(slots):
        below = from_below if slot == 0 else velocity[:, slot - 1]
        if slot + 1 < slots:
            above = jnp.where(slot + 1 < live_count, velocity[:, slot + 1], from_above)
        else:
            above = from_above
        feats = features(velocity[:, slot], below, above, inv_span[0, slot], kernels)
        proj = jnp.einsum("sczx,xk->sczk", feats, omega_stream, preferred_element_type=jnp.float32)
        table = lax.dynamic_index_in_dim(
            omega_table, omega_block[0, slot], 0, keepdims=False
        ).astype(jnp.float32)
        term = jnp.einsum("sczk,czk->sk", proj, table, precision=lax.Precision.HIGHEST)
        coef = coef + jnp.where(slot < live_count, term, jnp.zeros_like(term))
    coef = lax.psum(coef, "plane")
    snaps, comps, zw, xw = wall_shear.shape
    shear_f = (
        wall_shear.astype(jnp.float32)
        .reshape(snaps, comps, zw // 4, 4, xw // 4, 4)
        .mean(axis=(3, 5))
    )
    partial_sketch = jnp.einsum("smzx,sk->mzxk", shear_f, coef, precision=lax.Precision.HIGHEST)
    sketch = lax.psum_scatter(partial_sketch, "snap", scatter_dimension=2, tiled=True)
    total_rows = 2 * (X // 4) * (ZW // 4)
    flat = sketch.reshape(-1, sketch.shape[-1])
    local_gram = jnp.dot(flat.T, flat, precision=lax.Precision.HIGHEST)
    gram = lax.psum(local_gram, ("snap", "plane")) / jnp.float32(total_rows)
    return (sketch, gram)


def solution(mesh):
    return jax.shard_map(
        per_device,
        mesh=mesh,
        in_specs=(
            P("snap", "plane", None, None, None),
            P("plane"),
            P("plane", None),
            P(),
            P("plane", None),
            P(),
            P(),
            P("snap", None, "plane", None),
        ),
        out_specs=(P(None, "plane", "snap", None), P()),
        check_vma=False,
    )
```

profile of v0, /device:TPU:2, one launch (start us, length us, event | category | flops | bytes accessed | tf_op | source)
XLA Modules:
  0.0 790.4 jit_solution(1391584907513652331)
XLA Ops:
  7.9 1.2 fusion.21
  9.1 1.3 collective-permute-start
  10.4 3.0 collective-permute-start.1
  13.4 0.7 fusion.23
  19.2 0.2 slice_reduce_fusion.17
  19.5 0.1 reduce_sum.53
  19.6 0.1 reduce_sum.54
  22.2 1.3 add_bitcast_fusion.7
  23.6 1.3 add_bitcast_fusion.6
  24.9 0.7 fusion.22
  25.6 2.7 multiply_bitcast_fusion.3
  28.4 21.0 %reshape_reshape.12 = f32[9,32,4,32,4]{4,3,2,1,0:T(8,128)} reshape(f32[1,3,3,128,128]{4,3,2,1,0:T(8,128)S(1)} %copy.14) | data formatting | bytes 1179648 | tf_op jit(solution)/shard_map/reshape;reshape | solution.py:35
  49.5 7.9 %reduce_sum.55 = f32[9,32,32]{2,1,0:T(8,128)S(1)} reduce(f32[9,32,4,32,4]{4,3,2,1,0:T(8,128)} %reshape_reshape.12, f32[]{:T(128)} %constant.38.clone.1), dimensions={2,4}, to_apply=%region_2.3 | reduce | flops 138240 | bytes 626692 | tf_op jit(solution)/shard_map/reduce_sum | solution.py:35
  57.4 20.8 %reshape_reshape.13 = f32[9,32,4,32,4]{4,3,2,1,0:T(8,128)} reshape(f32[1,3,3,128,128]{4,3,2,1,0:T(8,128)S(1)} %copy.15) | data formatting | bytes 1179648 | tf_op jit(solution)/shard_map/reshape;reshape | solution.py:35
  78.3 7.9 %reduce_sum.56 = f32[9,32,32]{2,1,0:T(8,128)S(1)} reduce(f32[9,32,4,32,4]{4,3,2,1,0:T(8,128)} %reshape_reshape.13, f32[]{:T(128)} %constant.38.clone.1), dimensions={2,4}, to_apply=%region_3.4 | reduce | flops 138240 | bytes 626692 | tf_op jit(solution)/shard_map/reduce_sum | solution.py:35
  86.2 0.1 pad_maximum_fusion.2
  86.3 20.8 %reshape_reshape.14 = f32[9,32,4,32,4]{4,3,2,1,0:T(8,128)} reshape(f32[1,3,3,128,128]{4,3,2,1,0:T(8,128)S(1)} %copy.16) | data formatting | bytes 1179648 | tf_op jit(solution)/shard_map/reshape;reshape | solution.py:35
  107.2 7.9 %reduce_sum.57 = f32[9,32,32]{2,1,0:T(8,128)S(1)} reduce(f32[9,32,4,32,4]{4,3,2,1,0:T(8,128)} %reshape_reshape.14, f32[]{:T(128)} %constant.38.clone.1), dimensions={2,4}, to_apply=%region_4.5 | reduce | flops 138240 | bytes 626692 | tf_op jit(solution)/shard_map/reduce_sum | solution.py:35
  115.2 20.8 %reshape_reshape.15 = f32[9,32,4,32,4]{4,3,2,1,0:T(8,128)} reshape(f32[1,3,3,128,128]{4,3,2,1,0:T(8,128)S(1)} %copy.17) | data formatting | bytes 1179648 | tf_op jit(solution)/shard_map/reshape;reshape | solution.py:35
  136.0 8.0 %reduce_sum.58 = f32[9,32,32]{2,1,0:T(8,128)S(1)} reduce(f32[9,32,4,32,4]{4,3,2,1,0:T(8,128)} %reshape_reshape.15, f32[]{:T(128)} %constant.38.clone.1), dimensions={2,4}, to_apply=%region_5.6 | reduce | flops 138240 | bytes 626692 | tf_op jit(solution)/shard_map/reduce_sum | solution.py:35
  144.0 0.2 fusion.4
  144.2 0.2 fusion.5
  144.4 0.2 fusion.6
  144.6 0.2 fusion.7
  144.9 54.3 %psum.14 = f32[256]{0:T(256)S(1)} all-reduce(f32[256]{0:T(256)S(1)} %select_add_fusion), channel_id=1, replica_groups=mesh['snap'=16,'plane'=32] {'plane'}, use_global_device_ids=true, to_apply=%region_6.7 | all-reduce | flops 256 | bytes 2048 | tf_op jit(solution)/shard_map/psum | solution.py:61
  199.1 0.7 multiply_bitcast_fusion.4
  199.9 1.3 dynamic-slice
  201.8 109.0 %all-reduce.10.cloned.1.call-done = f32[2,1,32,256]{3,2,1,0:T(8,128)} async-done(((f32[2,1,32,256]{3,2,1,0:T(8,128)}), f32[2,1,32,256]{3,2,1,0:T(8,128)}) %all-reduce.10.cloned.1.call-update) | async-done | bytes 65552
  310.8 0.7 constant_dynamic-slice_fusion
  311.6 1.1 convolution_bitcast_fusion.4
  312.7 469.1 %all-reduce.8.cloned.1.call-done = f32[256,256]{1,0:T(8,128)} async-done(((f32[256,256]{1,0:T(8,128)}), f32[256,256]{1,0:T(8,128)}) %all-reduce.8.cloned.1.call-update) | async-done | bytes 262160 | tf_op jit(solution)/shard_map/psum | solution.py:73
  781.8 1.7 broadcast_multiply_fusion
  (30 shorter events, 0.4 us)
Async XLA Ops:
  7.2 136.9 %copy-start = (bf16[32,256]{1,0:T(8,128)(2,1)S(1)}, bf16[32,256]{1,0:T(8,128)(2,1)}, u32[]{:S(2)}) copy-start(bf16[32,256]{1,0:T(8,128)(2,1)} %param.14) | copy-start | bytes 49156
  7.2 6.3 copy-start.5
  7.2 12.0 %copy-start.3 = (f32[3,2,3,3]{3,1,2,0:T(2,128)S(1)}, f32[3,2,3,3]{3,1,2,0:T(2,128)}, u32[]{:S(2)}) copy-start(f32[3,2,3,3]{3,1,2,0:T(2,128)} %param.11) | copy-start | bytes 652
  7.2 12.3 %copy-start.7 = (bf16[1,2,4,128]{3,2,1,0:T(4,128)(2,1)S(1)}, bf16[1,2,4,128]{3,2,1,0:T(4,128)(2,1)}, u32[]{:S(2)}) copy-start(bf16[1,2,4,128]{3,2,1,0:T(4,128)(2,1)} %param.15) | copy-start | bytes 6148
  7.2 303.6 %all-reduce.10.cloned.1.call-start = ((), (), s32[]{:S(2)}) async-start(), calls=%async_computation.1 | async-start | bytes 131072
  9.1 16.5 %collective-permute-start = (bf16[1,3,128,128]{3,2,1,0:T(8,128)(2,1)S(1)}, bf16[1,3,128,128]{3,2,1,0:T(8,128)(2,1)S(1)}, u32[]{:S(2)}, u32[]{:S(2)}) collective-permute-start(bf16[1,3,128,128]{3,2,1,0:T(8,128)(2,1)S(1)} %get-tuple-element.29), channel_id=1, source_target_pairs={{1,0},{2,1},{3,2},{4,3},{5,4},{6,5},{7,6},{8,7},{9,8},{10,9},{11,1... | collective-permute-start | bytes 294920 | tf_op jit(solution)/shard_map/ppermute | solution.py:13
  10.4 15.2 %collective-permute-start.1 = (bf16[1,3,128,128]{3,2,1,0:T(8,128)(2,1)S(1)}, bf16[1,3,128,128]{3,2,1,0:T(8,128)(2,1)S(1)}, u32[]{:S(2)}, u32[]{:S(2)}) collective-permute-start(bf16[1,3,128,128]{3,2,1,0:T(8,128)(2,1)S(1)} %get-tuple-element.28), channel_id=1, source_target_pairs={{0,1},{1,2},{2,3},{3,4},{4,5},{5,6},{6,7},{7,8},{8,9},{9,10},{10,1... | collective-permute-start | bytes 294920 | tf_op jit(solution)/shard_map/ppermute | solution.py:13
  23.6 1.4 copy-start.6
  23.6 2.0 copy-start.1
  136.0 8.0 %copy-start.2 = (bf16[8,9,32,256]{3,2,1,0:T(8,128)(2,1)S(1)}, bf16[8,9,32,256]{3,2,1,0:T(8,128)(2,1)}, u32[]{:S(2)}) copy-start(bf16[8,9,32,256]{3,2,1,0:T(8,128)(2,1)} %param.13) | copy-start | bytes 3538948
  199.9 582.0 %all-reduce.8.cloned.1.call-start = ((), (), s32[]{:S(2)}) async-start(), calls=%async_computation | async-start | bytes 524288 | tf_op jit(solution)/shard_map/psum | solution.py:73
  311.6 471.9 %copy-start.4 = (f32[2,1,2,256]{3,2,1,0:T(2,128)}, f32[2,1,2,256]{3,2,1,0:T(2,128)S(1)}, u32[]{:S(2)}) copy-start(f32[2,1,2,256]{3,2,1,0:T(2,128)S(1)} %constant_dynamic-slice_fusion) | copy-start | bytes 12292
Sparse Core Ops, SparseCore 0:
  200.0 110.8 all-reduce.9
  316.9 464.9 all-reduce.7
where the time goes:
time: 791 us; the launch traced here: 790 us
  waiting for transfers between devices  578 us (73%)
  local copies, waits for them, and re-layouts  87.4 us (11%)
  blocking collectives  54.3 us (7%)
  other arithmetic  40.9 us (5%)
  between operations  23.3 us (3%)
    psum x1, waiting for transfers between devices, per_device(): gram = lax.psum(local_gram, ('snap', 'plane')) / jnp.float32(total_rows)  469 us
    unnamed x3, waiting for transfers between devices  109 us
    another operation x4, local copies, waits for them, and re-layouts, features(): filtered = grads.reshape(snaps, 9, zw // 4, 4, xw // 4, 4).mean(axis=(3, 5))  83.6 us
    psum x1, blocking collectives, per_device(): coef = lax.psum(coef, 'plane')  54.3 us
    reduce_sum x4, other arithmetic, features(): filtered = grads.reshape(snaps, 9, zw // 4, 4, xw // 4, 4).mean(axis=(3, 5))  31.8 us
  transfers between devices with their start and end apart: 4, of which 2 were waited for; matrix products, arithmetic and copies ran while one was open for 1% of the time, Pallas kernels for 0%

commit v1 on v0

--- a/solution.py
+++ b/solution.py
@@ -70,7 +70,7 @@
     total_rows = 2 * (X // 4) * (ZW // 4)
     flat = sketch.reshape(-1, sketch.shape[-1])
     local_gram = jnp.dot(flat.T, flat, precision=lax.Precision.HIGHEST)
-    gram = lax.psum(local_gram, ("snap", "plane")) / jnp.float32(total_rows)
+    gram = lax.psum(lax.psum(local_gram, "snap"), "plane") / jnp.float32(total_rows)
     return (sketch, gram)
 
 

time: 791 us -> 652 us (0.82)
  the two profiles are of different devices: /device:TPU:2 before, /device:TPU:1 now
where the time goes in v1:
time: 652 us
  waiting for transfers between devices  441 us (68%)
  local copies, waits for them, and re-layouts  87.4 us (13%)
  blocking collectives  47 us (7%)
  other arithmetic  40.9 us (6%)
  between operations  23 us (4%)
  starting transfers between devices  10.8 us (2%)
    psum x1, waiting for transfers between devices, per_device(): lax.psum(lax.psum(local_gram, 'snap'), 'plane') / jnp.float32(total_rows)  214 us
    psum x1, waiting for transfers between devices, per_device(): lax.psum(local_gram, 'snap')  117 us
    unnamed x4, waiting for transfers between devices  109 us
    another operation x4, local copies, waits for them, and re-layouts, features(): filtered = grads.reshape(snaps, 9, zw // 4, 4, xw // 4, 4).mean(axis=(3, 5))  83.6 us
    psum x1, blocking collectives, per_device(): coef = lax.psum(coef, 'plane')  47 us
    reduce_sum x4, other arithmetic, features(): filtered = grads.reshape(snaps, 9, zw // 4, 4, xw // 4, 4).mean(axis=(3, 5))  31.8 us
  transfers between devices with their start and end apart: 5, of which 3 were waited for; matrix products, arithmetic and copies ran while one was open for 1% of the time, Pallas kernels for 0%

profile of v1, /device:TPU:1, one launch (start us, length us, event | category | flops | bytes accessed | tf_op | source)
XLA Modules:
  0.0 651.6 jit_solution(2219740350577038557)
XLA Ops:
  7.9 1.2 fusion.21
  9.1 8.7 %collective-permute-start = (bf16[1,3,128,128]{3,2,1,0:T(8,128)(2,1)S(1)}, bf16[1,3,128,128]{3,2,1,0:T(8,128)(2,1)S(1)}, u32[]{:S(2)}, u32[]{:S(2)}) collective-permute-start(bf16[1,3,128,128]{3,2,1,0:T(8,128)(2,1)S(1)} %get-tuple-element.29), channel_id=1, source_target_pairs={{1,0},{2,1},{3,2},{4,3},{5,4},{6,5},{7,6},{8,7},{9,8},{10,9},{11,1... | collective-permute-start | bytes 294920 | tf_op jit(solution)/shard_map/ppermute | solution.py:13
  17.8 1.9 collective-permute-start.1
  19.8 0.7 fusion.23
  25.6 0.2 slice_reduce_fusion.17
  25.8 0.1 reduce_sum.53
  28.6 1.3 add_bitcast_fusion.7
  29.9 1.3 add_bitcast_fusion.6
  31.3 0.7 fusion.22
  32.0 2.7 multiply_bitcast_fusion.3
  34.8 21.0 %reshape_reshape.12 = f32[9,32,4,32,4]{4,3,2,1,0:T(8,128)} reshape(f32[1,3,3,128,128]{4,3,2,1,0:T(8,128)S(1)} %copy.14) | data formatting | bytes 1179648 | tf_op jit(solution)/shard_map/reshape;reshape | solution.py:35
  55.8 7.9 %reduce_sum.55 = f32[9,32,32]{2,1,0:T(8,128)S(1)} reduce(f32[9,32,4,32,4]{4,3,2,1,0:T(8,128)} %reshape_reshape.12, f32[]{:T(128)} %constant.38.clone.1), dimensions={2,4}, to_apply=%region_2.3 | reduce | flops 138240 | bytes 626692 | tf_op jit(solution)/shard_map/reduce_sum | solution.py:35
  63.8 20.8 %reshape_reshape.13 = f32[9,32,4,32,4]{4,3,2,1,0:T(8,128)} reshape(f32[1,3,3,128,128]{4,3,2,1,0:T(8,128)S(1)} %copy.15) | data formatting | bytes 1179648 | tf_op jit(solution)/shard_map/reshape;reshape | solution.py:35
  84.6 7.9 %reduce_sum.56 = f32[9,32,32]{2,1,0:T(8,128)S(1)} reduce(f32[9,32,4,32,4]{4,3,2,1,0:T(8,128)} %reshape_reshape.13, f32[]{:T(128)} %constant.38.clone.1), dimensions={2,4}, to_apply=%region_3.4 | reduce | flops 138240 | bytes 626692 | tf_op jit(solution)/shard_map/reduce_sum | solution.py:35
  92.5 0.1 pad_maximum_fusion.2
  92.7 20.8 %reshape_reshape.14 = f32[9,32,4,32,4]{4,3,2,1,0:T(8,128)} reshape(f32[1,3,3,128,128]{4,3,2,1,0:T(8,128)S(1)} %copy.16) | data formatting | bytes 1179648 | tf_op jit(solution)/shard_map/reshape;reshape | solution.py:35
  113.5 7.9 %reduce_sum.57 = f32[9,32,32]{2,1,0:T(8,128)S(1)} reduce(f32[9,32,4,32,4]{4,3,2,1,0:T(8,128)} %reshape_reshape.14, f32[]{:T(128)} %constant.38.clone.1), dimensions={2,4}, to_apply=%region_4.5 | reduce | flops 138240 | bytes 626692 | tf_op jit(solution)/shard_map/reduce_sum | solution.py:35
  121.5 20.8 %reshape_reshape.15 = f32[9,32,4,32,4]{4,3,2,1,0:T(8,128)} reshape(f32[1,3,3,128,128]{4,3,2,1,0:T(8,128)S(1)} %copy.17) | data formatting | bytes 1179648 | tf_op jit(solution)/shard_map/reshape;reshape | solution.py:35
  142.4 8.0 %reduce_sum.58 = f32[9,32,32]{2,1,0:T(8,128)S(1)} reduce(f32[9,32,4,32,4]{4,3,2,1,0:T(8,128)} %reshape_reshape.15, f32[]{:T(128)} %constant.38.clone.1), dimensions={2,4}, to_apply=%region_5.6 | reduce | flops 138240 | bytes 626692 | tf_op jit(solution)/shard_map/reduce_sum | solution.py:35
  150.4 0.2 fusion.4
  150.6 0.2 fusion.5
  150.8 0.2 fusion.6
  151.0 0.2 fusion.7
  151.2 47.0 %psum.21 = f32[256]{0:T(256)S(1)} all-reduce(f32[256]{0:T(256)S(1)} %select_add_fusion), channel_id=1, replica_groups=mesh['snap'=16,'plane'=32] {'plane'}, use_global_device_ids=true, to_apply=%region_6.7 | all-reduce | flops 256 | bytes 2048 | tf_op jit(solution)/shard_map/psum | solution.py:61
  198.2 0.7 multiply_bitcast_fusion.4
  199.0 1.3 dynamic-slice
  200.9 109.3 %all-reduce.13.cloned.1.call-done = f32[2,1,32,256]{3,2,1,0:T(8,128)} async-done(((f32[2,1,32,256]{3,2,1,0:T(8,128)}), f32[2,1,32,256]{3,2,1,0:T(8,128)}) %all-reduce.13.cloned.1.call-update) | async-done | bytes 65552
  310.2 0.7 constant_dynamic-slice_fusion
  310.9 1.1 convolution_bitcast_fusion.4
  312.1 116.8 %all-reduce.9.cloned.1.call-done = f32[256,256]{1,0:T(8,128)} async-done(((f32[256,256]{1,0:T(8,128)}), f32[256,256]{1,0:T(8,128)}) %all-reduce.9.cloned.1.call-update) | async-done | bytes 262160 | tf_op jit(solution)/shard_map/psum | solution.py:73
  429.0 214.4 %all-reduce.11.cloned.1.call-done = f32[256,256]{1,0:T(8,128)} async-done(((f32[256,256]{1,0:T(8,128)}), f32[256,256]{1,0:T(8,128)}) %all-reduce.11.cloned.1.call-update) | async-done | bytes 262160 | tf_op jit(solution)/shard_map/psum | solution.py:73
  643.4 1.7 broadcast_multiply_fusion
  (33 shorter events, 0.6 us)
Async XLA Ops:
  7.2 143.2 %copy-start = (bf16[32,256]{1,0:T(8,128)(2,1)S(1)}, bf16[32,256]{1,0:T(8,128)(2,1)}, u32[]{:S(2)}) copy-start(bf16[32,256]{1,0:T(8,128)(2,1)} %param.14) | copy-start | bytes 49156
  7.2 12.6 %copy-start.5 = (s32[1,4]{1,0:T(1,128)S(1)}, s32[1,4]{1,0:T(1,128)}, u32[]{:S(2)}) copy-start(s32[1,4]{1,0:T(1,128)} %param.12) | copy-start | bytes 52
  7.2 18.4 %copy-start.3 = (f32[3,2,3,3]{3,1,2,0:T(2,128)S(1)}, f32[3,2,3,3]{3,1,2,0:T(2,128)}, u32[]{:S(2)}) copy-start(f32[3,2,3,3]{3,1,2,0:T(2,128)} %param.11) | copy-start | bytes 652
  7.2 18.6 %copy-start.7 = (bf16[1,2,4,128]{3,2,1,0:T(4,128)(2,1)S(1)}, bf16[1,2,4,128]{3,2,1,0:T(4,128)(2,1)}, u32[]{:S(2)}) copy-start(bf16[1,2,4,128]{3,2,1,0:T(4,128)(2,1)} %param.15) | copy-start | bytes 6148
  7.2 303.0 %all-reduce.13.cloned.1.call-start = ((), (), s32[]{:S(2)}) async-start(), calls=%async_computation.2 | async-start | bytes 131072
  9.1 22.9 %collective-permute-start = (bf16[1,3,128,128]{3,2,1,0:T(8,128)(2,1)S(1)}, bf16[1,3,128,128]{3,2,1,0:T(8,128)(2,1)S(1)}, u32[]{:S(2)}, u32[]{:S(2)}) collective-permute-start(bf16[1,3,128,128]{3,2,1,0:T(8,128)(2,1)S(1)} %get-tuple-element.29), channel_id=1, source_target_pairs={{1,0},{2,1},{3,2},{4,3},{5,4},{6,5},{7,6},{8,7},{9,8},{10,9},{11,1... | collective-permute-start | bytes 294920 | tf_op jit(solution)/shard_map/ppermute | solution.py:13
  17.8 14.1 %collective-permute-start.1 = (bf16[1,3,128,128]{3,2,1,0:T(8,128)(2,1)S(1)}, bf16[1,3,128,128]{3,2,1,0:T(8,128)(2,1)S(1)}, u32[]{:S(2)}, u32[]{:S(2)}) collective-permute-start(bf16[1,3,128,128]{3,2,1,0:T(8,128)(2,1)S(1)} %get-tuple-element.28), channel_id=1, source_target_pairs={{0,1},{1,2},{2,3},{3,4},{4,5},{5,6},{6,7},{7,8},{8,9},{9,10},{10,1... | collective-permute-start | bytes 294920 | tf_op jit(solution)/shard_map/ppermute | solution.py:13
  29.9 1.4 copy-start.6
  29.9 2.0 copy-start.1
  142.3 8.0 %copy-start.2 = (bf16[8,9,32,256]{3,2,1,0:T(8,128)(2,1)S(1)}, bf16[8,9,32,256]{3,2,1,0:T(8,128)(2,1)}, u32[]{:S(2)}) copy-start(bf16[8,9,32,256]{3,2,1,0:T(8,128)(2,1)} %param.13) | copy-start | bytes 3538948
  198.9 230.1 %all-reduce.9.cloned.1.call-start = ((), (), s32[]{:S(2)}) async-start(), calls=%async_computation | async-start | bytes 524288 | tf_op jit(solution)/shard_map/psum | solution.py:73
  310.9 334.1 %copy-start.4 = (f32[2,1,2,256]{3,2,1,0:T(2,128)}, f32[2,1,2,256]{3,2,1,0:T(2,128)S(1)}, u32[]{:S(2)}) copy-start(f32[2,1,2,256]{3,2,1,0:T(2,128)S(1)} %constant_dynamic-slice_fusion) | copy-start | bytes 12292
  312.1 331.3 %all-reduce.11.cloned.1.call-start = ((), (), s32[]{:S(2)}) async-start(), calls=%async_computation.1 | async-start | bytes 524288 | tf_op jit(solution)/shard_map/psum | solution.py:73
Sparse Core Ops, SparseCore 0:
  199.0 111.1 all-reduce.12
  313.9 114.9 all-reduce.8
  431.3 212.0 all-reduce.10
